TPU v7x, 128 devices: a whole 4x4x4 slice. The times are simulated.
128 devices in a mesh: gy: 16 (over z_hi, x, core), gz: 8 (over z_lo, y).
Axes of the slice: x: 4, y: 4, z: 4 (z_hi: 2, z_lo: 2; z = z_hi * 2 + z_lo), core: 2. Of those that a mesh axis runs over, the one named last changes fastest.
Arguments:
- reference_image: bfloat16 [64, 1024, 4096], P(None, 'gy', 'gz'), may hold values from -6 to 6
- deformed: bfloat16 [64, 1024, 4096], P(None, 'gy', 'gz'), may hold values from -12 to 12
- displacement: bfloat16 [3, 64, 1024, 4096], P(None, None, 'gy', 'gz'), may hold values from -1 to 1
- plane_factors: float32 [2, 32, 8, 128], P(None, None, None, 'gy'), may hold values from -2.5 to 2.5
- depth_factors: float32 [2, 32, 4096], P(None, None, 'gz'), may hold values from -6 to 6
Outputs:
- residual: bfloat16 [64, 1024, 4096], P(None, 'gy', 'gz')
- step_plane: float32 [2, 32, 8, 128], P(None, None, None, 'gy')
- step_depth: float32 [2, 32, 4096], P(None, None, 'gz')
All inputs are finite; a program needn't handle non-finite values.
Results may differ from a plain program's by a relative error of at most 0.0004.
Values may be sent and summed in bfloat16 or wider, within the bound.
A program may use at most 256 MiB of HBM per device.

v0:
```python
import jax
import jax.numpy as jnp
from jax import lax
from jax.sharding import PartitionSpec as P

RANK = 32
KNOT = 8
epsilon = 1e-06
damping = 0.01
highest = lax.Precision.HIGHEST


def extended(cells, sides, width):
    for axis, dim in sides:
        count = lax.axis_size(axis)
        ends = count - 1
        head = lax.slice_in_dim(cells, 0, width, axis=dim)
        tail = lax.slice_in_dim(cells, cells.shape[dim] - width, cells.shape[dim], axis=dim)
        cells = jnp.concatenate(
            [
                lax.ppermute(tail, axis, [(i, (i + 1) % count) for i in range(ends)]),
                cells,
                lax.ppermute(head, axis, [((i + 1) % count, i) for i in range(ends)]),
            ],
            axis=dim,
        )
    return cells


def tent_weights(shift):
    moved = shift.astype(jnp.float32)
    return [jnp.maximum(0.0, 1.0 - jnp.abs(moved - offset)) for offset in (-1.0, 0.0, 1.0)]


def warp_image(padded, displacement):
    depth_x, width_y, width_z = displacement.shape[1:]
    weight_x = tent_weights(displacement[0])
    weight_y = tent_weights(displacement[1])
    weight_z = tent_weights(displacement[2])
    summed = jnp.zeros((depth_x, width_y, width_z), jnp.float32)
    for along_x in range(3):
        for along_y in range(3):
            partial_z = jnp.zeros((depth_x, width_y, width_z), jnp.float32)
            for along_z in range(3):
                window = padded[
                    along_x : along_x + depth_x,
                    along_y : along_y + width_y,
                    along_z : along_z + width_z,
                ]
                partial_z = partial_z + weight_z[along_z] * window.astype(jnp.float32)
            summed = summed + weight_x[along_x] * weight_y[along_y] * partial_z
    return summed


def expand_nodes(nodes):
    return jnp.repeat(jnp.repeat(nodes, KNOT, axis=2), KNOT, axis=3)


def reduce_nodes(field):
    leading = field.shape[:-2]
    depth_x, width_y = field.shape[-2:]
    shaped = field.reshape(leading + (depth_x // KNOT, KNOT, width_y // KNOT, KNOT))
    return jnp.sum(shaped, axis=(-3, -1))


def contract_rank(left, right):
    return lax.dot_general(left, right, (((0,), (0,)), ((), ())), precision=highest)


def contract_cells(left, right):
    return jnp.dot(left, right, precision=highest)


def contract_depth(left, right):
    return lax.dot_general(left, right, (((1,), (1,)), ((), ())), precision=highest)


def strip_terms(image, padded, displacement, plane_voxels, depth_factors):
    depth_x, width_y, width_z = image.shape
    cells = depth_x * width_y
    warped = warp_image(padded, displacement).reshape(cells, width_z)
    values = image.astype(jnp.float32).reshape(cells, width_z)
    flat_plane = plane_voxels.reshape(2, plane_voxels.shape[1], cells)
    contrast = contract_rank(flat_plane[0], depth_factors[0])
    brightness = contract_rank(flat_plane[1], depth_factors[1])
    misfit = warped - contrast * values - brightness
    product = misfit * values
    squares = values * values
    grad_depth = -jnp.stack(
        [contract_cells(flat_plane[0], product), contract_cells(flat_plane[1], misfit)]
    )
    level_sum = jnp.sum(flat_plane[1] * flat_plane[1], axis=1)
    first_depth = contract_cells(flat_plane[0] * flat_plane[0], squares)
    grad_voxels = -jnp.stack(
        [contract_depth(depth_factors[0], product), contract_depth(depth_factors[1], misfit)]
    )
    diag_voxels = contract_depth(depth_factors[0] * depth_factors[0], squares)
    grad_plane = reduce_nodes(grad_voxels.reshape(2, -1, depth_x, width_y))
    first_diag = reduce_nodes(diag_voxels.reshape(-1, depth_x, width_y))
    depth_level = KNOT * KNOT * jnp.sum(depth_factors[1] * depth_factors[1], axis=1)
    squared_sum = jnp.sum(misfit * misfit)
    residual = misfit.reshape(depth_x, width_y, width_z).astype(jnp.bfloat16)
    return (
        residual,
        squared_sum,
        grad_plane,
        first_diag,
        depth_level,
        grad_depth,
        first_depth,
        level_sum,
    )


def local(reference_image, deformed, displacement, plane_factors, depth_factors):
    rimmed = extended(deformed, (("gy", 1), ("gz", 2)), 1)
    padded = jnp.pad(rimmed, ((1, 1), (0, 0), (0, 0)))
    plane_voxels = expand_nodes(plane_factors)
    (
        residual,
        local_energy,
        grad_plane,
        first_diag,
        depth_level,
        grad_depth,
        first_depth,
        level_sum,
    ) = strip_terms(reference_image, padded, displacement, plane_voxels, depth_factors)
    nodes_x = plane_factors.shape[2]
    nodes_y = plane_factors.shape[3] * lax.axis_size("gy")
    full_z = depth_factors.shape[2] * lax.axis_size("gz")
    energy = lax.psum(local_energy, ("gy", "gz"))
    grad_plane, first_diag, depth_level = lax.psum((grad_plane, first_diag, depth_level), "gz")
    diag_plane = jnp.stack(
        [first_diag, jnp.broadcast_to(depth_level[:, None, None], first_diag.shape)]
    )
    lam_plane = damping * RANK * energy / (nodes_x * nodes_y)
    lam_depth = damping * energy / full_z
    step_plane = -grad_plane / (diag_plane + lam_plane + epsilon)
    grad_depth, first_depth, level_sum = lax.psum((grad_depth, first_depth, level_sum), "gy")
    diag_depth = jnp.stack([first_depth, jnp.broadcast_to(level_sum[:, None], first_depth.shape)])
    step_depth = -grad_depth / (diag_depth + lam_depth + epsilon)
    return (residual, step_plane, step_depth)


def solution(mesh):
    placed = (
        P(None, "gy", "gz"),
        P(None, "gy", "gz"),
        P(None, None, "gy", "gz"),
        P(None, None, None, "gy"),
        P(None, None, "gz"),
    )
    return jax.shard_map(
        local,
        mesh=mesh,
        in_specs=placed,
        out_specs=(P(None, "gy", "gz"), P(None, None, None, "gy"), P(None, None, "gz")),
        check_vma=False,
    )
```

profile of v0, /device:TPU:7, one launch (start us, length us, event | category | flops | bytes accessed | tf_op | source)
XLA Modules:
  0.0 613.2 jit_solution(7184010167852653225)
XLA Ops:
  7.2 0.0 all-reduce.5.cloned.1.call-start
  7.2 1.4 fusion.133
  8.7 6.0 collective-permute-start
  14.7 0.0 copy-start.4
  14.7 2.2 collective-permute-start.1
  16.9 9.0 %fusion.132 = (bf16[1,64,64,512]{3,2,1,0:T(8,128)(2,1)}, bf16[1,64,64,512]{3,2,1,0:T(8,128)(2,1)}, bf16[1,64,64,512]{3,2,1,0:T(8,128)(2,1)}) fusion(bf16[3,64,64,512]{3,2,1,0:T(8,128)(2,1)} %param.7), kind=kLoop, calls=%fused_computation.173 | loop fusion | bytes 25165824 | tf_op jit(solution)/shard_map/slice | solution.py:39
  25.9 0.1 fusion.122
  26.1 0.3 broadcast_in_dim.28
  26.4 8.8 %fusion.124 = f32[4096,512]{1,0:T(8,128)} fusion(f32[32,4096]{0,1:T(8,128)S(1)} %bitcast.293, f32[2,32,512]{2,1,0:T(8,128)S(1)} %copy-done.5), kind=kOutput, calls=%fused_computation.159 | convolution fusion | flops 805306368 | bytes 10551296 | tf_op jit(solution)/shard_map/dot_general | solution.py:67
  35.2 1.2 convert_multiply_fusion
  36.5 7.4 %convolution_reduce_fusion = f32[32,8,8]{0,2,1:T(8,128)} fusion(f32[8,8,8,8,512]{4,3,2,1,0:T(8,128)S(1)} %bitcast.291, f32[2,32,512]{2,1,0:T(8,128)S(1)} %copy-done.5), kind=kOutput, calls=%fused_computation.139 | convolution fusion | flops 805451776 | bytes 8462336 | tf_op jit(solution)/shard_map/dot_general | solution.py:75
  43.9 0.3 broadcast_in_dim.34
  44.2 5.7 convolution_bitcast_fusion.2
  49.8 0.5 broadcast_multiply_fusion
  50.4 13.0 %copy.49 = bf16[64,64,512]{1,0,2:T(8,128)(2,1)} copy(bf16[64,64,512]{2,1,0:T(8,128)(2,1)} %param.6) | data formatting | bytes 8388608 | tf_op args[1]
  63.4 0.2 copy.59
  63.5 12.7 %copy.48 = bf16[64,1,512]{1,0,2:T(8,128)(2,1)} copy(bf16[64,1,512]{2,0,1:T(8,128)(2,1)S(1)} %collective-permute-done) | data formatting | bytes 131072 | tf_op jit(solution)/shard_map/ppermute | solution.py:21
  76.2 12.7 %copy.50 = bf16[64,1,512]{1,0,2:T(8,128)(2,1)} copy(bf16[64,1,512]{2,0,1:T(8,128)(2,1)S(1)} %collective-permute-done.1) | data formatting | bytes 131072 | tf_op jit(solution)/shard_map/ppermute | solution.py:23
  88.9 0.9 pad_maximum_fusion.5
  89.8 3.2 collective-permute-start.2
  93.0 1.3 collective-permute-start.3
  94.3 0.3 broadcast_reduce_fusion
  94.6 13.4 %copy.61 = bf16[1,64,64,512]{2,1,3,0:T(8,128)(2,1)} copy(bf16[1,64,64,512]{3,2,1,0:T(8,128)(2,1)} %get-tuple-element.14) | data formatting | bytes 8388608
  108.0 13.0 %copy.62 = bf16[1,64,64,512]{2,1,3,0:T(8,128)(2,1)} copy(bf16[1,64,64,512]{3,2,1,0:T(8,128)(2,1)} %get-tuple-element.13) | data formatting | bytes 8388608
  121.0 12.9 %copy.63 = bf16[1,64,64,512]{2,1,3,0:T(8,128)(2,1)} copy(bf16[1,64,64,512]{3,2,1,0:T(8,128)(2,1)} %get-tuple-element.12) | data formatting | bytes 8388608
  133.9 32.9 %psum.55 = f32[32]{0:T(128)S(1)} all-reduce(f32[32]{0:T(128)S(1)} %broadcast_reduce_fusion), channel_id=1, replica_groups=mesh['gy'=16,'gz'=8] {'gy'}, use_global_device_ids=true, to_apply=%region_11.12 | all-reduce | flops 32 | bytes 256 | tf_op jit(solution)/shard_map/psum | solution.py:140
  166.8 24.1 %maximum_maximum_fusion = (bf16[64,66,513]{1,0,2:T(8,128)(2,1)S(1)}, bf16[64,66,513]{1,0,2:T(8,128)(2,1)}) fusion(bf16[64,1,512]{1,0,2:T(8,128)(2,1)} %copy.50, bf16[64,64,512]{1,0,2:T(8,128)(2,1)} %copy.49, bf16[64,1,512]{1,0,2:T(8,128)(2,1)} %copy.48, bf16[64,66,1]{1,0,2:T(8,128)(2,1)S(1)} %collective-permute-done.2, ...), kind=kLoop, calls=%fused_computation.126 | loop fusion | flops 34670592 | bytes 13009920 | tf_op jit(solution)/shard_map/concatenate | solution.py:19
  190.8 24.0 %select_maximum_fusion = bf16[66,66,514]{1,0,2:T(8,128)(2,1)S(1)} fusion(bf16[64,66,1]{1,0,2:T(8,128)(2,1)S(1)} %collective-permute-done.3, bf16[64,66,1]{1,0,2:T(8,128)(2,1)S(1)} %collective-permute-done.2, bf16[64,1,512]{1,0,2:T(8,128)(2,1)} %copy.50, bf16[64,64,512]{1,0,2:T(8,128)(2,1)} %copy.49, bf16[64,1,512]{1,0,2:T(8,128)(2,1)} %copy.48), kind=kLoop, calls=%fused_computation.119 | loop fusion | flops 40301712 | bytes 8820240 | tf_op jit(solution)/shard_map/concatenate | solution.py:19
  214.8 119.0 %fusion.15 = f32[64,64,512]{1,0,2:T(8,128)} fusion(bf16[1,64,64,512]{2,1,3,0:T(8,128)(2,1)} %copy.61, bf16[1,64,64,512]{2,1,3,0:T(8,128)(2,1)} %copy.62, bf16[1,64,64,512]{2,1,3,0:T(8,128)(2,1)} %copy.63, bf16[64,64,512]{1,0,2:T(8,128)(2,1)} %copy.49, bf16[66,66,514]{1,0,2:T(8,128)(2,1)S(1)} %select_maximum_fusion, ...), kind=kLoop, calls=%fused_computation.26 | loop fusion | flops 293601280 | bytes 125960192 | tf_op jit(solution)/shard_map/add | solution.py:51
  333.9 12.7 %copy.56 = f32[64,64,512]{2,1,0:T(8,128)} copy(f32[64,64,512]{1,0,2:T(8,128)} %fusion.15) | data formatting | bytes 16777216 | tf_op jit(solution)/shard_map/add | solution.py:51
  346.6 1.6 broadcast_in_dim.32
  348.3 17.3 %multiply_reduce_fusion = (f32[]{:T(128)}, f32[4096,512]{1,0:T(8,128)}, bf16[4096,512]{1,0:T(8,128)(2,1)}, f32[4096,512]{1,0:T(8,128)S(1)}) fusion(bf16[64,64,512]{2,1,0:T(8,128)(2,1)} %param.5, f32[32,4096]{0,1:T(8,128)} %bitcast.295, f32[2,32,512]{2,1,0:T(8,128)S(1)} %copy-done.5, f32[4096,512]{1,0:T(8,128)} %fusion.124, f32[64,64,512]{2,1,0:T(8,128)} %copy.56), kind=kOutput, calls=%fused_computation.135 | convolution fusion | flops 822083584 | bytes 42532868 | tf_op jit(solution)/shard_map/dot_general | solution.py:67
  365.6 10.2 %convolution_bitcast_fusion.4 = f32[1,32,512]{2,1,0:T(8,128)S(1)} fusion(f32[4096,512]{1,0:T(8,128)} %get-tuple-element.16, f32[32,4096]{0,1:T(8,128)S(1)} %bitcast.294), kind=kOutput, calls=%fused_computation.142 | convolution fusion | flops 805306368 | bytes 8978432 | tf_op jit(solution)/shard_map/dot_general | solution.py:71
  375.8 7.7 %convolution_bitcast_fusion.1 = f32[32,4096]{1,0:T(8,128)S(1)} fusion(f32[4096,512]{1,0:T(8,128)S(1)} %copy-done, f32[2,32,512]{2,1,0:T(8,128)S(1)} %copy-done.5), kind=kOutput, calls=%fused_computation.137 | convolution fusion | flops 805306368 | bytes 8978432 | tf_op jit(solution)/shard_map/dot_general | solution.py:75
  383.5 0.0 copy-start.6
  383.6 5.3 convolution_bitcast_fusion.3
  388.8 8.0 %convolution_bitcast_fusion = f32[32,4096]{1,0:T(8,128)S(1)} fusion(f32[4096,512]{1,0:T(8,128)S(1)} %get-tuple-element.22, f32[2,32,512]{2,1,0:T(8,128)S(1)} %copy-done.5), kind=kOutput, calls=%fused_computation.136 | convolution fusion | flops 805306368 | bytes 8978432 | tf_op jit(solution)/shard_map/dot_general | solution.py:75
  396.8 68.7 %psum.52 = f32[]{:T(128)} all-reduce(f32[]{:T(128)} %get-tuple-element.15), channel_id=1, replica_groups=mesh['gy'=16,'gz'=8] {'gy','gz'}, use_global_device_ids=true, to_apply=%region_7.8 | all-reduce | flops 1 | bytes 8 | tf_op jit(solution)/shard_map/psum | solution.py:132
  465.5 0.6 copy.57
  466.1 2.0 copy.58
  468.1 2.2 maximum_reduce_fusion
  471.6 0.7 maximum_negate_fusion
  472.3 0.0 all-reduce.5.cloned.1.call-update
  472.3 26.1 %all-reduce.2 = (f32[32]{0:T(128)S(1)}, f32[1,32,8,8]{1,3,2,0:T(8,128)S(1)}, f32[2,32,8,8]{1,3,2,0:T(8,128)S(1)}) all-reduce(f32[32]{0:T(128)S(1)} %copy-done.8, f32[1,32,8,8]{1,3,2,0:T(8,128)S(1)} %bitcast.303, f32[2,32,8,8]{1,3,2,0:T(8,128)S(1)} %neg.13), channel_id=1, replica_groups=mesh['gy'=16,'gz'=8] {'gz'}, use_global_device_ids=true, to_apply=%region_5.6 | all-reduce | flops 6176 | bytes 49408 | tf_op jit(solution)/shard_map/psum | solution.py:133
  498.4 0.7 fusion.118
  499.1 105.1 %all-reduce.5.cloned.1.call-done = (f32[1,32,512]{2,1,0:T(8,128)}, f32[2,32,512]{2,1,0:T(8,128)}) async-done(((f32[1,32,512]{2,1,0:T(8,128)}, f32[2,32,512]{2,1,0:T(8,128)}), (f32[1,32,512]{2,1,0:T(8,128)}, f32[2,32,512]{2,1,0:T(8,128)})) %all-reduce.5.cloned.1.call-update) | async-done | bytes 196624 | tf_op jit(solution)/shard_map/psum | solution.py:140
  604.2 0.1 stack_broadcast_in_dim.5
  604.2 1.6 fusion.116
  (28 shorter events, 0.2 us)
Async XLA Ops:
  7.2 18.8 %copy-start.7 = (f32[2,32,8,8]{1,3,2,0:T(8,128)S(1)}, f32[2,32,8,8]{1,3,2,0:T(8,128)}, u32[]{:S(2)}) copy-start(f32[2,32,8,8]{1,3,2,0:T(8,128)} %param.8) | copy-start | bytes 49156
  7.2 18.8 %copy-start.5 = (f32[2,32,512]{2,1,0:T(8,128)S(1)}, f32[2,32,512]{2,1,0:T(8,128)}, u32[]{:S(2)}) copy-start(f32[2,32,512]{2,1,0:T(8,128)} %param.9) | copy-start | bytes 393220
  7.2 597.0 %all-reduce.5.cloned.1.call-start = ((), (), s32[]{:S(2)}) async-start(), calls=%async_computation | async-start | bytes 393216 | tf_op jit(solution)/shard_map/psum | solution.py:140
  8.7 54.8 %collective-permute-start = (bf16[64,1,512]{2,0,1:T(8,128)(2,1)S(1)}, bf16[64,1,512]{2,0,1:T(8,128)(2,1)S(1)}, u32[]{:S(2)}, u32[]{:S(2)}) collective-permute-start(bf16[64,1,512]{2,0,1:T(8,128)(2,1)S(1)} %copy.64), channel_id=1, source_target_pairs={{0,8},{8,16},{16,24},{24,32},{32,40},{40,48},{48,56},{56,64},{64,7... | collective-permute-start | bytes 196616 | tf_op jit(solution)/shard_map/ppermute | solution.py:21
  14.7 20.5 %copy-start.4 = (bf16[64,64,512]{2,1,0:T(8,128)(2,1)S(1)}, bf16[64,64,512]{2,1,0:T(8,128)(2,1)}, u32[]{:S(2)}) copy-start(bf16[64,64,512]{2,1,0:T(8,128)(2,1)} %param.5) | copy-start | bytes 12582916
  14.7 61.5 %collective-permute-start.1 = (bf16[64,1,512]{2,0,1:T(8,128)(2,1)S(1)}, bf16[64,1,512]{2,0,1:T(8,128)(2,1)S(1)}, u32[]{:S(2)}, u32[]{:S(2)}) collective-permute-start(bf16[64,1,512]{2,0,1:T(8,128)(2,1)S(1)} %copy.65), channel_id=1, source_target_pairs={{8,0},{16,8},{24,16},{32,24},{40,32},{48,40},{56,48},{64,56},{72,6... | collective-permute-start | bytes 196616 | tf_op jit(solution)/shard_map/ppermute | solution.py:23
  26.4 8.8 %copy-start.1 = (f32[32,64,8,8]{0,3,2,1:T(8,128)}, f32[32,64,8,8]{0,3,2,1:T(8,128)S(1)}, u32[]{:S(2)}) copy-start(f32[32,64,8,8]{0,3,2,1:T(8,128)S(1)} %broadcast_in_dim.28) | copy-start | bytes 1572868
  89.8 77.0 %collective-permute-start.2 = (bf16[64,66,1]{1,0,2:T(8,128)(2,1)S(1)}, bf16[64,66,1]{1,0,2:T(8,128)(2,1)S(1)}, u32[]{:S(2)}, u32[]{:S(2)}) collective-permute-start(bf16[64,66,1]{1,0,2:T(8,128)(2,1)S(1)} %get-tuple-element.10), channel_id=1, source_target_pairs={{0,1},{1,2},{2,3},{3,4},{4,5},{5,6},{6,7},{8,9},{9,10},{10,11},{11... | collective-permute-start | bytes 25352 | tf_op jit(solution)/shard_map/ppermute | solution.py:21
  93.0 73.8 %collective-permute-start.3 = (bf16[64,66,1]{1,0,2:T(8,128)(2,1)S(1)}, bf16[64,66,1]{1,0,2:T(8,128)(2,1)S(1)}, u32[]{:S(2)}, u32[]{:S(2)}) collective-permute-start(bf16[64,66,1]{1,0,2:T(8,128)(2,1)S(1)} %get-tuple-element.11), channel_id=1, source_target_pairs={{1,0},{2,1},{3,2},{4,3},{5,4},{6,5},{7,6},{9,8},{10,9},{11,10},{12... | collective-permute-start | bytes 25352 | tf_op jit(solution)/shard_map/ppermute | solution.py:23
  348.3 17.3 %copy-start.2 = (f32[32,64,8,8]{0,3,2,1:T(8,128)S(1)}, f32[32,64,8,8]{0,3,2,1:T(8,128)}, u32[]{:S(2)}) copy-start(f32[32,64,8,8]{0,3,2,1:T(8,128)} %copy-done.1) | copy-start | bytes 1572868
  365.6 10.2 %copy-start = (f32[4096,512]{1,0:T(8,128)S(1)}, f32[4096,512]{1,0:T(8,128)}, u32[]{:S(2)}) copy-start(f32[4096,512]{1,0:T(8,128)} %get-tuple-element.16) | copy-start | bytes 25165828
  365.6 18.0 %copy-start.3 = (f32[32,64,8,8]{0,3,2,1:T(8,128)S(1)}, f32[32,64,8,8]{0,3,2,1:T(8,128)}, u32[]{:S(2)}) copy-start(f32[32,64,8,8]{0,3,2,1:T(8,128)} %broadcast_in_dim.32) | copy-start | bytes 1572868
  383.5 88.8 %copy-start.6 = (f32[32,8,8]{0,2,1:T(8,128)S(1)}, f32[32,8,8]{0,2,1:T(8,128)}, u32[]{:S(2)}) copy-start(f32[32,8,8]{0,2,1:T(8,128)} %convolution_reduce_fusion) | copy-start | bytes 24580
  383.5 88.8 %copy-start.8 = (f32[32]{0:T(128)S(1)}, f32[32]{0:T(128)}, u32[]{:S(2)}) copy-start(f32[32]{0:T(128)} %broadcast_multiply_fusion) | copy-start | bytes 388
Sparse Core Ops, SparseCore 0:
  472.4 131.7 all-reduce.4
where the time goes:
time: 621 us; the launch traced here: 613 us
  other arithmetic  175 us (28%)
  blocking collectives  128 us (21%)
  local copies, waits for them, and re-layouts  106 us (17%)
  waiting for transfers between devices  105 us (17%)
  matrix products  70.4 us (11%)
  between operations  16.1 us (3%)
  starting transfers between devices  12.7 us (2%)
    add x1, other arithmetic, warp_image(): summed = summed + weight_x[along_x] * weight_y[along_y] * partial_z  119 us
    psum x1, waiting for transfers between devices, local(): lax.psum((grad_depth, first_depth, level_sum), 'gy')  105 us
    psum x1, blocking collectives, local(): energy = lax.psum(local_energy, ('gy', 'gz'))  68.7 us
    unnamed x24, local copies, waits for them, and re-layouts  52.3 us
    concatenate x2, other arithmetic, extended(): jnp.concatenate([lax.ppermute(tail, axis, [(i, (i + 1) % count) for i in...  48.1 us
    psum x1, blocking collectives, local(): lax.psum((grad_depth, first_depth, level_sum), 'gy')  32.9 us
    psum x1, blocking collectives, local(): lax.psum((grad_plane, first_diag, depth_level), 'gz')  26.1 us
    dot_general x2, matrix products, contract_rank(): lax.dot_general(left, right, (((0,), (0,)), ((), ())), precision=highest)  26.1 us
  transfers between devices with their start and end apart: 5, of which 1 were waited for; matrix products, arithmetic and copies ran while one was open for 16% of the time, Pallas kernels for 0%

commit v1 on v0

--- a/solution.py
+++ b/solution.py
@@ -1,3 +1,4 @@
+import functools
 import jax
 import jax.numpy as jnp
 from jax import lax
@@ -8,6 +9,13 @@
 epsilon = 1e-06
 damping = 0.01
 highest = lax.Precision.HIGHEST
+
+
+def advance_works(inputs, shard_axis, along_axis):
+    return jax.lax.psum(jax.lax.psum(inputs, along_axis), shard_axis)
+
+
+spot_meet = functools.partial(advance_works, shard_axis="gy", along_axis="gz")
 
 
 def extended(cells, sides, width):
@@ -129,7 +137,7 @@
     nodes_x = plane_factors.shape[2]
     nodes_y = plane_factors.shape[3] * lax.axis_size("gy")
     full_z = depth_factors.shape[2] * lax.axis_size("gz")
-    energy = lax.psum(local_energy, ("gy", "gz"))
+    energy = spot_meet(local_energy)
     grad_plane, first_diag, depth_level = lax.psum((grad_plane, first_diag, depth_level), "gz")
     diag_plane = jnp.stack(
         [first_diag, jnp.broadcast_to(depth_level[:, None, None], first_diag.shape)]

time: 621 us -> 591 us (0.952)
  blocking collectives: 128 us -> 70.5 us
  waiting for transfers between devices: 105 us -> 132 us
    psum x2 -> x1, blocking collectives: 102 us -> 41.7 us  [advance_works(): return jax.lax.psum(jax.lax.psum(inputs, along_axis), shard_axis)]
    psum x1, waiting for transfers between devices: 105 us -> 132 us  [local(): lax.psum((grad_depth, first_depth, level_sum), 'gy')]
  transfers between devices with their start and end apart: 5 -> 5, of which waited for: 1 -> 1; matrix products, arithmetic and copies ran while one was open for 16% -> 17% of each run, Pallas kernels for 0% -> 0%
where the time goes in v1:
time: 591 us; the launch traced here: 583 us
  other arithmetic  176 us (30%)
  waiting for transfers between devices  132 us (22%)
  local copies, waits for them, and re-layouts  106 us (18%)
  matrix products  70.8 us (12%)
  blocking collectives  70.5 us (12%)
  between operations  15.9 us (3%)
  starting transfers between devices  12.7 us (2%)
    psum x1, waiting for transfers between devices, local(): lax.psum((grad_depth, first_depth, level_sum), 'gy')  132 us
    add x1, other arithmetic, warp_image(): summed = summed + weight_x[along_x] * weight_y[along_y] * partial_z  119 us
    unnamed x24, local copies, waits for them, and re-layouts  52.1 us
    concatenate x2, other arithmetic, extended(): jnp.concatenate([lax.ppermute(tail, axis, [(i, (i + 1) % count) for i in...  48.3 us
    psum x1, blocking collectives, advance_works(): return jax.lax.psum(jax.lax.psum(inputs, along_axis), shard_axis)  41.7 us
    psum x1, blocking collectives, local(): lax.psum((grad_plane, first_diag, depth_level), 'gz')  28.8 us
    dot_general x2, matrix products, contract_rank(): lax.dot_general(left, right, (((0,), (0,)), ((), ())), precision=highest)  26.5 us
    dot_general x3, matrix products, contract_depth(): lax.dot_general(left, right, (((1,), (1,)), ((), ())), precision=highest)  23.1 us
  transfers between devices with their start and end apart: 5, of which 1 were waited for; matrix products, arithmetic and copies ran while one was open for 17% of the time, Pallas kernels for 0%

profile of v1, /device:TPU:7, one launch (start us, length us, event | category | flops | bytes accessed | tf_op | source)
XLA Modules:
  0.0 583.4 jit_solution(7792110212231260446)
XLA Ops:
  7.2 0.0 all-reduce.6.cloned.1.call-start
  7.2 1.4 fusion.133
  8.7 6.0 %collective-permute-start = (bf16[64,1,512]{2,0,1:T(8,128)(2,1)S(1)}, bf16[64,1,512]{2,0,1:T(8,128)(2,1)S(1)}, u32[]{:S(2)}, u32[]{:S(2)}) collective-permute-start(bf16[64,1,512]{2,0,1:T(8,128)(2,1)S(1)} %copy.64), channel_id=1, source_target_pairs={{0,8},{8,16},{16,24},{24,32},{32,40},{40,48},{48,56},{56,64},{64,7... | collective-permute-start | bytes 196616 | tf_op jit(solution)/shard_map/ppermute | solution.py:29
  14.7 0.0 copy-start.4
  14.7 2.2 collective-permute-start.1
  16.9 9.0 %fusion.132 = (bf16[1,64,64,512]{3,2,1,0:T(8,128)(2,1)}, bf16[1,64,64,512]{3,2,1,0:T(8,128)(2,1)}, bf16[1,64,64,512]{3,2,1,0:T(8,128)(2,1)}) fusion(bf16[3,64,64,512]{3,2,1,0:T(8,128)(2,1)} %param.7), kind=kLoop, calls=%fused_computation.173 | loop fusion | bytes 25165824 | tf_op jit(solution)/shard_map/slice | solution.py:47
  25.9 0.1 fusion.122
  26.1 0.3 broadcast_in_dim.28
  26.4 8.8 %fusion.124 = f32[4096,512]{1,0:T(8,128)} fusion(f32[32,4096]{0,1:T(8,128)S(1)} %bitcast.293, f32[2,32,512]{2,1,0:T(8,128)S(1)} %copy-done.5), kind=kOutput, calls=%fused_computation.159 | convolution fusion | flops 805306368 | bytes 10551296 | tf_op jit(solution)/shard_map/dot_general | solution.py:75
  35.2 1.2 convert_multiply_fusion
  36.4 7.5 %convolution_reduce_fusion = f32[32,8,8]{0,2,1:T(8,128)} fusion(f32[8,8,8,8,512]{4,3,2,1,0:T(8,128)S(1)} %bitcast.291, f32[2,32,512]{2,1,0:T(8,128)S(1)} %copy-done.5), kind=kOutput, calls=%fused_computation.139 | convolution fusion | flops 805451776 | bytes 8462336 | tf_op jit(solution)/shard_map/dot_general | solution.py:83
  43.9 0.3 broadcast_in_dim.34
  44.2 5.7 convolution_bitcast_fusion.2
  49.9 0.6 broadcast_multiply_fusion
  50.4 13.0 %copy.49 = bf16[64,64,512]{1,0,2:T(8,128)(2,1)} copy(bf16[64,64,512]{2,1,0:T(8,128)(2,1)} %param.6) | data formatting | bytes 8388608 | tf_op args[1]
  63.4 0.2 copy.59
  63.6 0.0 collective-permute-done
  63.6 12.7 %copy.48 = bf16[64,1,512]{1,0,2:T(8,128)(2,1)} copy(bf16[64,1,512]{2,0,1:T(8,128)(2,1)S(1)} %collective-permute-done) | data formatting | bytes 131072 | tf_op jit(solution)/shard_map/ppermute | solution.py:29
  76.2 12.7 %copy.50 = bf16[64,1,512]{1,0,2:T(8,128)(2,1)} copy(bf16[64,1,512]{2,0,1:T(8,128)(2,1)S(1)} %collective-permute-done.1) | data formatting | bytes 131072 | tf_op jit(solution)/shard_map/ppermute | solution.py:31
  88.9 0.9 pad_maximum_fusion.5
  89.8 3.2 collective-permute-start.2
  93.0 1.3 collective-permute-start.3
  94.3 0.3 broadcast_reduce_fusion
  94.7 13.2 %copy.61 = bf16[1,64,64,512]{2,1,3,0:T(8,128)(2,1)} copy(bf16[1,64,64,512]{3,2,1,0:T(8,128)(2,1)} %get-tuple-element.17) | data formatting | bytes 8388608
  107.8 13.0 %copy.62 = bf16[1,64,64,512]{2,1,3,0:T(8,128)(2,1)} copy(bf16[1,64,64,512]{3,2,1,0:T(8,128)(2,1)} %get-tuple-element.16) | data formatting | bytes 8388608
  120.8 12.9 %copy.63 = bf16[1,64,64,512]{2,1,3,0:T(8,128)(2,1)} copy(bf16[1,64,64,512]{3,2,1,0:T(8,128)(2,1)} %get-tuple-element.15) | data formatting | bytes 8388608
  133.7 24.1 %maximum_maximum_fusion = (bf16[64,66,513]{1,0,2:T(8,128)(2,1)S(1)}, bf16[64,66,513]{1,0,2:T(8,128)(2,1)}) fusion(bf16[64,1,512]{1,0,2:T(8,128)(2,1)} %copy.50, bf16[64,64,512]{1,0,2:T(8,128)(2,1)} %copy.49, bf16[64,1,512]{1,0,2:T(8,128)(2,1)} %copy.48, bf16[64,66,1]{1,0,2:T(8,128)(2,1)S(1)} %collective-permute-done.2, ...), kind=kLoop, calls=%fused_computation.126 | loop fusion | flops 34670592 | bytes 13009920 | tf_op jit(solution)/shard_map/concatenate | solution.py:27
  157.8 24.2 %select_maximum_fusion = bf16[66,66,514]{1,0,2:T(8,128)(2,1)S(1)} fusion(bf16[64,66,1]{1,0,2:T(8,128)(2,1)S(1)} %collective-permute-done.3, bf16[64,66,1]{1,0,2:T(8,128)(2,1)S(1)} %collective-permute-done.2, bf16[64,1,512]{1,0,2:T(8,128)(2,1)} %copy.50, bf16[64,64,512]{1,0,2:T(8,128)(2,1)} %copy.49, bf16[64,1,512]{1,0,2:T(8,128)(2,1)} %copy.48), kind=kLoop, calls=%fused_computation.119 | loop fusion | flops 40301712 | bytes 8820240 | tf_op jit(solution)/shard_map/concatenate | solution.py:27
  182.1 118.9 %fusion.15 = f32[64,64,512]{1,0,2:T(8,128)} fusion(bf16[1,64,64,512]{2,1,3,0:T(8,128)(2,1)} %copy.61, bf16[1,64,64,512]{2,1,3,0:T(8,128)(2,1)} %copy.62, bf16[1,64,64,512]{2,1,3,0:T(8,128)(2,1)} %copy.63, bf16[64,64,512]{1,0,2:T(8,128)(2,1)} %copy.49, bf16[66,66,514]{1,0,2:T(8,128)(2,1)S(1)} %select_maximum_fusion, ...), kind=kLoop, calls=%fused_computation.26 | loop fusion | flops 293601280 | bytes 125960192 | tf_op jit(solution)/shard_map/add | solution.py:59
  301.0 12.7 %copy.56 = f32[64,64,512]{2,1,0:T(8,128)} copy(f32[64,64,512]{1,0,2:T(8,128)} %fusion.15) | data formatting | bytes 16777216 | tf_op jit(solution)/shard_map/add | solution.py:59
  313.8 1.6 broadcast_in_dim.32
  315.4 17.8 %multiply_reduce_fusion = (f32[]{:T(128)}, f32[4096,512]{1,0:T(8,128)}, bf16[4096,512]{1,0:T(8,128)(2,1)}, f32[4096,512]{1,0:T(8,128)S(1)}) fusion(bf16[64,64,512]{2,1,0:T(8,128)(2,1)} %param.5, f32[32,4096]{0,1:T(8,128)} %bitcast.295, f32[2,32,512]{2,1,0:T(8,128)S(1)} %copy-done.5, f32[4096,512]{1,0:T(8,128)} %fusion.124, f32[64,64,512]{2,1,0:T(8,128)} %copy.56), kind=kOutput, calls=%fused_computation.135 | convolution fusion | flops 822083584 | bytes 42532868 | tf_op jit(solution)/shard_map/dot_general | solution.py:75
  333.2 10.2 %convolution_bitcast_fusion.4 = f32[1,32,512]{2,1,0:T(8,128)S(1)} fusion(f32[4096,512]{1,0:T(8,128)} %get-tuple-element.19, f32[32,4096]{0,1:T(8,128)S(1)} %bitcast.294), kind=kOutput, calls=%fused_computation.142 | convolution fusion | flops 805306368 | bytes 8978432 | tf_op jit(solution)/shard_map/dot_general | solution.py:79
  343.3 7.7 %convolution_bitcast_fusion.1 = f32[32,4096]{1,0:T(8,128)S(1)} fusion(f32[4096,512]{1,0:T(8,128)S(1)} %copy-done, f32[2,32,512]{2,1,0:T(8,128)S(1)} %copy-done.5), kind=kOutput, calls=%fused_computation.137 | convolution fusion | flops 805306368 | bytes 8978432 | tf_op jit(solution)/shard_map/dot_general | solution.py:83
  351.1 0.0 copy-start.6
  351.1 5.3 convolution_bitcast_fusion.3
  356.4 7.9 %convolution_bitcast_fusion = f32[32,4096]{1,0:T(8,128)S(1)} fusion(f32[4096,512]{1,0:T(8,128)S(1)} %get-tuple-element.25, f32[2,32,512]{2,1,0:T(8,128)S(1)} %copy-done.5), kind=kOutput, calls=%fused_computation.136 | convolution fusion | flops 805306368 | bytes 8978432 | tf_op jit(solution)/shard_map/dot_general | solution.py:83
  364.3 0.6 copy.57
  364.9 1.9 copy.58
  366.9 2.2 maximum_reduce_fusion
  369.1 28.8 %all-reduce.3 = (f32[32]{0:T(128)S(1)}, f32[1,32,8,8]{1,3,2,0:T(8,128)S(1)}, f32[2,32,8,8]{1,3,2,0:T(8,128)S(1)}, f32[]{:T(128)}) all-reduce(f32[32]{0:T(128)S(1)} %copy-done.8, f32[1,32,8,8]{1,3,2,0:T(8,128)S(1)} %bitcast.303, f32[2,32,8,8]{1,3,2,0:T(8,128)S(1)} %neg.13, f32[]{:T(128)} %get-tuple-element.18), channel_id=1, replica_groups=mesh['gy'=16,'gz'=8] {'gz'}, use_global_device_ids=true, to_apply=%region_5.6 | all-reduce | flops 6177 | bytes 49416 | tf_op jit(solution)/shard_map/psum | solution.py:141
  398.0 41.7 %all-reduce.1 = (f32[]{:T(128)}, f32[32]{0:T(128)S(1)}) all-reduce(f32[]{:T(128)} %get-tuple-element.10, f32[32]{0:T(128)S(1)} %broadcast_reduce_fusion), channel_id=1, replica_groups=mesh['gy'=16,'gz'=8] {'gy'}, use_global_device_ids=true, to_apply=%region_8.9 | all-reduce | flops 33 | bytes 264 | tf_op jit(solution)/shard_map/psum | solution.py:15
  440.9 0.7 maximum_negate_fusion
  441.6 0.0 all-reduce.6.cloned.1.call-update
  441.6 0.7 fusion.118
  442.3 132.4 %all-reduce.6.cloned.1.call-done = (f32[1,32,512]{2,1,0:T(8,128)}, f32[2,32,512]{2,1,0:T(8,128)}) async-done(((f32[1,32,512]{2,1,0:T(8,128)}, f32[2,32,512]{2,1,0:T(8,128)}), (f32[1,32,512]{2,1,0:T(8,128)}, f32[2,32,512]{2,1,0:T(8,128)})) %all-reduce.6.cloned.1.call-update) | async-done | bytes 196624 | tf_op jit(solution)/shard_map/psum | solution.py:148
  574.7 0.1 stack_broadcast_in_dim.5
  574.7 1.6 fusion.116
  (27 shorter events, 0.2 us)
Async XLA Ops:
  7.2 18.8 %copy-start.7 = (f32[2,32,8,8]{1,3,2,0:T(8,128)S(1)}, f32[2,32,8,8]{1,3,2,0:T(8,128)}, u32[]{:S(2)}) copy-start(f32[2,32,8,8]{1,3,2,0:T(8,128)} %param.8) | copy-start | bytes 49156
  7.2 18.8 %copy-start.5 = (f32[2,32,512]{2,1,0:T(8,128)S(1)}, f32[2,32,512]{2,1,0:T(8,128)}, u32[]{:S(2)}) copy-start(f32[2,32,512]{2,1,0:T(8,128)} %param.9) | copy-start | bytes 393220
  7.2 567.5 %all-reduce.6.cloned.1.call-start = ((), (), s32[]{:S(2)}) async-start(), calls=%async_computation | async-start | bytes 393216 | tf_op jit(solution)/shard_map/psum | solution.py:148
  8.7 54.9 %collective-permute-start = (bf16[64,1,512]{2,0,1:T(8,128)(2,1)S(1)}, bf16[64,1,512]{2,0,1:T(8,128)(2,1)S(1)}, u32[]{:S(2)}, u32[]{:S(2)}) collective-permute-start(bf16[64,1,512]{2,0,1:T(8,128)(2,1)S(1)} %copy.64), channel_id=1, source_target_pairs={{0,8},{8,16},{16,24},{24,32},{32,40},{40,48},{48,56},{56,64},{64,7... | collective-permute-start | bytes 196616 | tf_op jit(solution)/shard_map/ppermute | solution.py:29
  14.7 20.5 %copy-start.4 = (bf16[64,64,512]{2,1,0:T(8,128)(2,1)S(1)}, bf16[64,64,512]{2,1,0:T(8,128)(2,1)}, u32[]{:S(2)}) copy-start(bf16[64,64,512]{2,1,0:T(8,128)(2,1)} %param.5) | copy-start | bytes 12582916
  14.7 61.5 %collective-permute-start.1 = (bf16[64,1,512]{2,0,1:T(8,128)(2,1)S(1)}, bf16[64,1,512]{2,0,1:T(8,128)(2,1)S(1)}, u32[]{:S(2)}, u32[]{:S(2)}) collective-permute-start(bf16[64,1,512]{2,0,1:T(8,128)(2,1)S(1)} %copy.65), channel_id=1, source_target_pairs={{8,0},{16,8},{24,16},{32,24},{40,32},{48,40},{56,48},{64,56},{72,6... | collective-permute-start | bytes 196616 | tf_op jit(solution)/shard_map/ppermute | solution.py:31
  26.4 8.8 %copy-start.1 = (f32[32,64,8,8]{0,3,2,1:T(8,128)}, f32[32,64,8,8]{0,3,2,1:T(8,128)S(1)}, u32[]{:S(2)}) copy-start(f32[32,64,8,8]{0,3,2,1:T(8,128)S(1)} %broadcast_in_dim.28) | copy-start | bytes 1572868
  89.8 43.9 %collective-permute-start.2 = (bf16[64,66,1]{1,0,2:T(8,128)(2,1)S(1)}, bf16[64,66,1]{1,0,2:T(8,128)(2,1)S(1)}, u32[]{:S(2)}, u32[]{:S(2)}) collective-permute-start(bf16[64,66,1]{1,0,2:T(8,128)(2,1)S(1)} %get-tuple-element.13), channel_id=1, source_target_pairs={{0,1},{1,2},{2,3},{3,4},{4,5},{5,6},{6,7},{8,9},{9,10},{10,11},{11... | collective-permute-start | bytes 25352 | tf_op jit(solution)/shard_map/ppermute | solution.py:29
  93.0 40.7 %collective-permute-start.3 = (bf16[64,66,1]{1,0,2:T(8,128)(2,1)S(1)}, bf16[64,66,1]{1,0,2:T(8,128)(2,1)S(1)}, u32[]{:S(2)}, u32[]{:S(2)}) collective-permute-start(bf16[64,66,1]{1,0,2:T(8,128)(2,1)S(1)} %get-tuple-element.14), channel_id=1, source_target_pairs={{1,0},{2,1},{3,2},{4,3},{5,4},{6,5},{7,6},{9,8},{10,9},{11,10},{12... | collective-permute-start | bytes 25352 | tf_op jit(solution)/shard_map/ppermute | solution.py:31
  315.4 17.8 %copy-start.2 = (f32[32,64,8,8]{0,3,2,1:T(8,128)S(1)}, f32[32,64,8,8]{0,3,2,1:T(8,128)}, u32[]{:S(2)}) copy-start(f32[32,64,8,8]{0,3,2,1:T(8,128)} %copy-done.1) | copy-start | bytes 1572868
  333.2 10.2 %copy-start = (f32[4096,512]{1,0:T(8,128)S(1)}, f32[4096,512]{1,0:T(8,128)}, u32[]{:S(2)}) copy-start(f32[4096,512]{1,0:T(8,128)} %get-tuple-element.19) | copy-start | bytes 25165828
  333.2 17.9 %copy-start.3 = (f32[32,64,8,8]{0,3,2,1:T(8,128)S(1)}, f32[32,64,8,8]{0,3,2,1:T(8,128)}, u32[]{:S(2)}) copy-start(f32[32,64,8,8]{0,3,2,1:T(8,128)} %broadcast_in_dim.32) | copy-start | bytes 1572868
  351.1 18.0 %copy-start.6 = (f32[32,8,8]{0,2,1:T(8,128)S(1)}, f32[32,8,8]{0,2,1:T(8,128)}, u32[]{:S(2)}) copy-start(f32[32,8,8]{0,2,1:T(8,128)} %convolution_reduce_fusion) | copy-start | bytes 24580
  351.1 18.0 %copy-start.8 = (f32[32]{0:T(128)S(1)}, f32[32]{0:T(128)}, u32[]{:S(2)}) copy-start(f32[32]{0:T(128)} %broadcast_multiply_fusion) | copy-start | bytes 388
Sparse Core Ops, SparseCore 0:
  441.7 132.8 all-reduce.5
